TPU v7x, 128 devices: a whole 4x4x4 slice. The times are simulated.
128 devices in a mesh: grp: 4 (over x), seq: 32 (over y, z, core).
Axes of the slice: x: 4, y: 4, z: 4, core: 2. Of those that a mesh axis runs over, the one named last changes fastest.
Arguments:
- grad_output: bfloat16 [4096, 8192], P('seq', 'grp'), may hold values from -6 to 6
- hidden: bfloat16 [4096, 28672], P('seq', 'grp'), may hold values from -6 to 6
- down_weight: bfloat16 [28672, 8192], P('seq', 'grp'), may hold values from -0.0625 to 0.0625
- adapter_down: bfloat16 [64, 64, 28672], P(None, None, ('grp', 'seq')), may hold values from -0.03125 to 0.03125
- adapter_up: bfloat16 [64, 64, 8192], P(None, None, ('grp', 'seq')), may hold values from -0.0625 to 0.0625
- job_tenant: int32 [32, 4], replicated, may hold values from 0 to 63, all different within a row
- job_count: int32 [32, 4], replicated, may hold values from 1 to 64, 128 in all within a row
Outputs:
- grad_hidden: bfloat16 [4096, 28672], P('seq', 'grp')
- grad_adapter_down: float32 [64, 64, 28672], P(None, None, ('grp', 'seq'))
- grad_adapter_up: float32 [64, 64, 8192], P(None, None, ('grp', 'seq'))
Inputs may be any that keep to these rules, and one draw needn't show every extreme that they name: `job_tenant`: each row names 4 different tenants; every tenant is named by some row. `job_count`: each row sums to 128, and its largest entry is exactly 64.
All inputs are finite; a program needn't handle non-finite values.
Results may differ from a plain program's by a relative error of at most 0.015.
Values may be sent and summed in bfloat16 or wider, within the bound.
A program may use at most 128 MiB of HBM per device.

v0:
```python
import jax
import jax.numpy as jnp
from jax import lax
from jax.sharding import PartitionSpec as P

ADAPTER_SCALE = 2.0


def shards(grad_output, hidden, down_weight, adapter_down, adapter_up, job_tenant, job_count):
    shard_index = lax.axis_index("seq")
    shard_count = lax.axis_size("seq")
    group_count = lax.axis_size("grp")
    tok_rows = grad_output.shape[0]
    job_slots = job_tenant.shape[1]
    ranks = adapter_down.shape[1]
    down_slab = adapter_down.shape[2]
    up_slab = adapter_up.shape[2]
    tenant_total = adapter_down.shape[0]
    contract_last = (((1,), (1,)), ((), ()))
    contract_rows = (((0,), (0,)), ((), ()))
    tenant_table = (
        job_tenant[:, :, None] == lax.broadcasted_iota(jnp.int32, (1, 1, tenant_total), 2)
    ).astype(jnp.float32)
    totals = jnp.sum(job_count.astype(jnp.float32)[:, :, None] * tenant_table, axis=(0, 1))
    weights = ADAPTER_SCALE / totals
    table_here = lax.dynamic_index_in_dim(tenant_table, shard_index, 0, keepdims=False)
    job_weights = jnp.sum(table_here * weights[None, :], axis=1)
    counts_here = lax.dynamic_index_in_dim(job_count, shard_index, 0, keepdims=False)
    run_ends = jnp.cumsum(counts_here)
    run_starts = run_ends - counts_here
    positions = lax.broadcasted_iota(jnp.int32, (tok_rows, job_slots), 0)
    member = ((positions >= run_starts[None, :]) & (positions < run_ends[None, :])).astype(
        jnp.float32
    )
    chosen = job_tenant.T
    fetched_down, fetched_up = (
        lax.all_to_all(adapter_down[chosen], "seq", split_axis=1, concat_axis=3, tiled=True),
        lax.all_to_all(adapter_up[chosen], "seq", split_axis=1, concat_axis=3, tiled=True),
    )
    down_stack = fetched_down.reshape(job_slots * ranks, shard_count * down_slab)
    up_stack = fetched_up.reshape(job_slots * ranks, shard_count * up_slab)

    def select_jobs(projected):
        return jnp.sum(projected.reshape(tok_rows, job_slots, ranks) * member[:, :, None], axis=1)

    grad_proj = lax.dot_general(
        grad_output, up_stack, contract_last, preferred_element_type=jnp.float32
    )
    act_proj = lax.dot_general(
        hidden, down_stack, contract_last, preferred_element_type=jnp.float32
    )
    rank_part = jnp.concatenate([select_jobs(grad_proj), select_jobs(act_proj)], axis=1).astype(
        jnp.bfloat16
    )
    partial_value = lax.dot_general(
        lax.all_gather(grad_output, "seq", axis=0, tiled=True),
        down_weight,
        contract_last,
        preferred_element_type=jnp.float32,
    )
    routed = lax.all_to_all(
        partial_value.astype(jnp.bfloat16), "seq", split_axis=0, concat_axis=1, tiled=True
    )
    width_here = routed.shape[1] // group_count
    packed = jnp.concatenate(
        [
            routed.reshape(tok_rows, group_count, width_here),
            jnp.broadcast_to(rank_part[:, None, :], (tok_rows, group_count, 2 * ranks)),
        ],
        axis=2,
    )
    summed = lax.psum_scatter(
        lax.optimization_barrier(packed).astype(jnp.float32).astype(jnp.bfloat16),
        "grp",
        scatter_dimension=1,
        tiled=True,
    ).astype(jnp.float32)
    base_grad = summed[:, 0, :width_here].astype(jnp.bfloat16)
    rank_sum = summed[:, 0, width_here:]
    grad_rank = rank_sum[:, :ranks].astype(jnp.bfloat16)
    act_rank = rank_sum[:, ranks:].astype(jnp.bfloat16)
    grad_spread = (
        (member[:, :, None] * lax.optimization_barrier(grad_rank).astype(jnp.float32)[:, None, :])
        .reshape(tok_rows, job_slots * ranks)
        .astype(jnp.bfloat16)
    )
    act_spread = (
        (member[:, :, None] * lax.optimization_barrier(act_rank).astype(jnp.float32)[:, None, :])
        .reshape(tok_rows, job_slots * ranks)
        .astype(jnp.bfloat16)
    )
    adapter_term = (
        jnp.dot(grad_spread, down_stack, preferred_element_type=jnp.float32) * ADAPTER_SCALE
    )
    grad_hidden = (base_grad.astype(jnp.float32) + adapter_term).astype(jnp.bfloat16)
    down_rows = lax.dot_general(
        grad_spread, hidden, contract_rows, preferred_element_type=jnp.float32
    )
    down_rows = (down_rows.reshape(job_slots, ranks, -1) * job_weights[:, None, None]).astype(
        jnp.bfloat16
    )
    up_rows = lax.dot_general(
        act_spread, grad_output, contract_rows, preferred_element_type=jnp.float32
    )
    up_rows = (up_rows.reshape(job_slots, ranks, -1) * job_weights[:, None, None]).astype(
        jnp.bfloat16
    )
    returned_down, returned_up = (
        lax.all_to_all(
            down_rows.reshape(job_slots, ranks, shard_count, down_slab),
            "seq",
            split_axis=2,
            concat_axis=1,
            tiled=True,
        ),
        lax.all_to_all(
            up_rows.reshape(job_slots, ranks, shard_count, up_slab),
            "seq",
            split_axis=2,
            concat_axis=1,
            tiled=True,
        ),
    )
    tenant_map = (
        tenant_table.transpose(1, 0, 2)
        .reshape(job_slots * shard_count, tenant_total)
        .astype(jnp.bfloat16)
    )
    grad_adapter_down = lax.dot_general(
        tenant_map,
        returned_down.reshape(job_slots * shard_count, ranks * down_slab),
        contract_rows,
        preferred_element_type=jnp.float32,
    ).reshape(tenant_total, ranks, down_slab)
    grad_adapter_up = lax.dot_general(
        tenant_map,
        returned_up.reshape(job_slots * shard_count, ranks * up_slab),
        contract_rows,
        preferred_element_type=jnp.float32,
    ).reshape(tenant_total, ranks, up_slab)
    return (grad_hidden, grad_adapter_down, grad_adapter_up)


def solution(mesh):
    placed = (
        P("seq", "grp"),
        P("seq", "grp"),
        P("seq", "grp"),
        P(None, None, ("grp", "seq")),
        P(None, None, ("grp", "seq")),
        P(),
        P(),
    )
    return jax.shard_map(
        shards,
        mesh=mesh,
        in_specs=placed,
        out_specs=(P("seq", "grp"), P(None, None, ("grp", "seq")), P(None, None, ("grp", "seq"))),
        check_vma=False,
    )
```

profile of v0, /device:TPU:32, one launch (start us, length us, event | category | flops | bytes accessed | tf_op | source)
XLA Modules:
  0.0 503.5 jit_solution(17961774575114402384)
XLA Ops:
  15.2 4.6 reshape.175
  19.9 8.2 %all-to-all-start.1 = ((bf16[32,2,8192]{2,1,0:T(2,128)(2,1)}), bf16[32,2,8192]{2,1,0:T(2,128)(2,1)S(1)}, u32[]{:S(2)}, u32[]{:S(2)}) async-start(bf16[32,2,8192]{2,1,0:T(2,128)(2,1)} %reshape.175), calls=%async_computation.1 | async-start | bytes 2097152 | tf_op jit(solution)/shard_map/all_to_all | solution.py:38
  30.9 4.8 copy.92
  35.7 11.5 %all-to-all-done.1 = bf16[32,2,8192]{2,1,0:T(2,128)(2,1)S(1)} async-done(((bf16[32,2,8192]{2,1,0:T(2,128)(2,1)}), bf16[32,2,8192]{2,1,0:T(2,128)(2,1)S(1)}, u32[]{:S(2)}, u32[]{:S(2)}) %all-to-all-start.1) | async-done | bytes 1048608 | tf_op jit(solution)/shard_map/all_to_all | solution.py:38
  47.3 6.3 %all-to-all-start.2 = ((bf16[4,32,64,224]{3,2,0,1:T(8,128)(2,1)}), bf16[4,32,64,224]{3,2,0,1:T(8,128)(2,1)}, u32[]{:S(2)}, u32[]{:S(2)}) async-start(bf16[4,32,64,224]{3,2,0,1:T(8,128)(2,1)} %copy.92), calls=%async_computation.2 | async-start | bytes 8388608 | tf_op jit(solution)/shard_map/all_to_all | solution.py:37
  53.6 83.7 %all-gather.2.cloned.1.call-done = bf16[4096,2048]{1,0:T(8,128)(2,1)} async-done(((bf16[128,2048]{1,0:T(8,128)(2,1)}), bf16[4096,2048]{1,0:T(8,128)(2,1)}) %all-gather.2.cloned.1.call-update) | async-done | bytes 16777232 | tf_op jit(solution)/shard_map/all_gather | solution.py:56
  137.2 23.3 %convolution_convert_fusion = bf16[4096,896]{1,0:T(8,128)(2,1)} fusion(bf16[4096,2048]{1,0:T(8,128)(2,1)} %all-gather.2.cloned.1.call-done, bf16[896,2048]{1,0:T(8,128)(2,1)} %param.9), kind=kOutput, calls=%fused_computation.8 | convolution fusion | flops 15036055552 | bytes 27787264 | tf_op jit(solution)/shard_map/dot_general | solution.py:55
  160.5 10.8 %copy.88 = bf16[32,128,896]{1,2,0:T(8,128)(2,1)} copy(bf16[32,128,896]{2,1,0:T(8,128)(2,1)} %bitcast.114) | data formatting | bytes 14680064 | tf_op jit(solution)/shard_map/all_to_all | solution.py:61
  171.3 6.8 %all-to-all-start = ((bf16[32,128,896]{1,2,0:T(8,128)(2,1)}), bf16[32,128,896]{1,2,0:T(8,128)(2,1)}, u32[]{:S(2)}, u32[]{:S(2)}) async-start(bf16[32,128,896]{1,2,0:T(8,128)(2,1)} %copy.88), calls=%async_computation | async-start | bytes 14680064 | tf_op jit(solution)/shard_map/all_to_all | solution.py:61
  186.0 6.6 %copy.93 = bf16[4,1,64,32,224]{4,3,2,0,1:T(8,128)(2,1)} copy(bf16[4,1,64,32,224]{4,2,0,3,1:T(8,128)(2,1)} %bitcast.15) | data formatting | bytes 7340032 | tf_op jit(solution)/shard_map/all_to_all | solution.py:37
  192.7 9.0 %reshape.145 = bf16[256,7168]{1,0:T(8,128)(2,1)} reshape(bf16[4,1,64,32,224]{4,3,2,0,1:T(8,128)(2,1)} %copy.93) | data formatting | bytes 7340032 | tf_op jit(solution)/shard_map/reshape | solution.py:40
  204.8 82.1 %all-to-all-done = bf16[32,128,896]{1,2,0:T(8,128)(2,1)} async-done(((bf16[32,128,896]{1,2,0:T(8,128)(2,1)}), bf16[32,128,896]{1,2,0:T(8,128)(2,1)}, u32[]{:S(2)}, u32[]{:S(2)}) %all-to-all-start) | async-done | bytes 7340064 | tf_op jit(solution)/shard_map/all_to_all | solution.py:61
  286.9 6.5 %pad_maximum_fusion = bf16[128,4,7296]{0,2,1:T(8,128)(2,1)} fusion(bf16[128,4,128]{0,2,1:T(8,128)(2,1)S(1)} %broadcast_in_dim.5, bf16[128,4,7168]{0,2,1:T(8,128)(2,1)} %bitcast.2), kind=kLoop, calls=%fused_computation.7 | loop fusion | flops 14942208 | bytes 14942208 | tf_op jit(solution)/shard_map/concatenate | solution.py:65
  294.5 73.3 %reduce-scatter.2.cloned.1.call-done = bf16[128,1,7296]{0,2,1:T(8,128)(2,1)} async-done(((bf16[128,4,7296]{0,2,1:T(8,128)(2,1)}), bf16[128,1,7296]{0,2,1:T(8,128)(2,1)}) %reduce-scatter.2.cloned.1.call-update) | async-done | bytes 1867792 | tf_op jit(solution)/shard_map/reduce_scatter | solution.py:72
  375.5 4.9 reshape.177
  380.4 7.5 %all-to-all-start.4 = ((bf16[32,2,8192]{2,1,0:T(2,128)(2,1)}), bf16[32,2,8192]{2,1,0:T(2,128)(2,1)S(1)}, u32[]{:S(2)}, u32[]{:S(2)}) async-start(bf16[32,2,8192]{2,1,0:T(2,128)(2,1)} %reshape.177), calls=%async_computation.5 | async-start | bytes 2097152 | tf_op jit(solution)/shard_map/all_to_all | solution.py:116
  390.8 8.8 %reshape.147 = bf16[4,64,32,224]{3,2,1,0:T(8,128)(2,1)} reshape(bf16[4,64,7168]{2,1,0:T(8,128)(2,1)} %fusion) | data formatting | bytes 7340032 | tf_op jit(solution)/shard_map/reshape | solution.py:110
  399.6 6.5 %copy.95 = bf16[4,64,32,224]{3,1,0,2:T(8,128)(2,1)} copy(bf16[4,64,32,224]{3,2,1,0:T(8,128)(2,1)} %reshape.147) | data formatting | bytes 7340032 | tf_op jit(solution)/shard_map/reshape | solution.py:110
  406.2 7.8 %all-to-all-start.3 = ((bf16[4,64,32,224]{3,1,0,2:T(8,128)(2,1)}), bf16[4,64,32,224]{3,1,0,2:T(8,128)(2,1)}, u32[]{:S(2)}, u32[]{:S(2)}) async-start(bf16[4,64,32,224]{3,1,0,2:T(8,128)(2,1)} %copy.95), calls=%async_computation.4 | async-start | bytes 8388608 | tf_op jit(solution)/shard_map/all_to_all | solution.py:109
  430.8 37.3 %all-to-all-done.3 = bf16[4,64,32,224]{3,1,0,2:T(8,128)(2,1)} async-done(((bf16[4,64,32,224]{3,1,0,2:T(8,128)(2,1)}), bf16[4,64,32,224]{3,1,0,2:T(8,128)(2,1)}, u32[]{:S(2)}, u32[]{:S(2)}) %all-to-all-start.3) | async-done | bytes 3670048 | tf_op jit(solution)/shard_map/all_to_all | solution.py:109
  468.1 4.8 copy.96
  472.9 8.5 %reshape.148 = bf16[128,14336]{1,0:T(8,128)(2,1)} reshape(bf16[4,32,64,1,224]{4,2,1,0,3:T(8,128)(2,1)} %copy.96) | data formatting | bytes 7340032 | tf_op jit(solution)/shard_map/reshape | solution.py:131
  481.4 6.0 %copy.97 = bf16[14336,128]{1,0:T(8,128)(2,1)} copy(bf16[14336,128]{0,1:T(8,128)(2,1)} %bitcast.110) | data formatting | bytes 7340032 | tf_op jit(solution)/shard_map/dot_general | solution.py:129
  487.4 4.5 fusion.14
  (66 shorter events, 54.7 us)
Async XLA Ops:
  7.2 20.9 %copy-start = (bf16[64,64,224]{2,1,0:T(8,128)(2,1)S(1)}, bf16[64,64,224]{2,1,0:T(8,128)(2,1)}, u32[]{:S(2)}) copy-start(bf16[64,64,224]{2,1,0:T(8,128)(2,1)} %param.10) | copy-start | bytes 5505028
  7.2 130.0 %all-gather.2.cloned.1.call-start = ((), (), s32[]{:S(2)}) async-start(), calls=%async_computation.6 | async-start | bytes 17301504 | tf_op jit(solution)/shard_map/all_gather | solution.py:56
  19.9 27.4 %all-to-all-start.1 = ((bf16[32,2,8192]{2,1,0:T(2,128)(2,1)}), bf16[32,2,8192]{2,1,0:T(2,128)(2,1)S(1)}, u32[]{:S(2)}, u32[]{:S(2)}) async-start(bf16[32,2,8192]{2,1,0:T(2,128)(2,1)} %reshape.175), calls=%async_computation.1 | async-start | bytes 2097152 | tf_op jit(solution)/shard_map/all_to_all | solution.py:38
  47.3 124.0 %all-to-all-start.2 = ((bf16[4,32,64,224]{3,2,0,1:T(8,128)(2,1)}), bf16[4,32,64,224]{3,2,0,1:T(8,128)(2,1)}, u32[]{:S(2)}, u32[]{:S(2)}) async-start(bf16[4,32,64,224]{3,2,0,1:T(8,128)(2,1)} %copy.92), calls=%async_computation.2 | async-start | bytes 8388608 | tf_op jit(solution)/shard_map/all_to_all | solution.py:37
  171.2 7.4 %copy-start.6 = (s32[32,4]{0,1:T(4,128)S(1)}, s32[32,4]{0,1:T(4,128)}, u32[]{:S(2)}) copy-start(s32[32,4]{0,1:T(4,128)} %param.13) | copy-start | bytes 1540
  171.3 115.6 %all-to-all-start = ((bf16[32,128,896]{1,2,0:T(8,128)(2,1)}), bf16[32,128,896]{1,2,0:T(8,128)(2,1)}, u32[]{:S(2)}, u32[]{:S(2)}) async-start(bf16[32,128,896]{1,2,0:T(8,128)(2,1)} %copy.88), calls=%async_computation | async-start | bytes 14680064 | tf_op jit(solution)/shard_map/all_to_all | solution.py:61
  178.1 189.8 %reduce-scatter.2.cloned.1.call-start = ((), (), s32[]{:S(2)}) async-start(), calls=%async_computation.7 | async-start | bytes 9338880 | tf_op jit(solution)/shard_map/reduce_scatter | solution.py:72
  180.6 3.8 copy-start.4
  192.7 9.0 %copy-start.2 = (bf16[128,7168]{1,0:T(8,128)(2,1)S(1)}, bf16[128,7168]{1,0:T(8,128)(2,1)}, u32[]{:S(2)}) copy-start(bf16[128,7168]{1,0:T(8,128)(2,1)} %param.8) | copy-start | bytes 5505028
  293.5 0.7 copy-start.5
  375.5 12.4 %copy-start.3 = (bf16[128,7168]{1,0:T(8,128)(2,1)S(1)}, bf16[128,7168]{1,0:T(8,128)(2,1)}, u32[]{:S(2)}) copy-start(bf16[128,7168]{1,0:T(8,128)(2,1)} %param.8) | copy-start | bytes 5505028
  380.4 25.8 %all-to-all-start.4 = ((bf16[32,2,8192]{2,1,0:T(2,128)(2,1)}), bf16[32,2,8192]{2,1,0:T(2,128)(2,1)S(1)}, u32[]{:S(2)}, u32[]{:S(2)}) async-start(bf16[32,2,8192]{2,1,0:T(2,128)(2,1)} %reshape.177), calls=%async_computation.5 | async-start | bytes 2097152 | tf_op jit(solution)/shard_map/all_to_all | solution.py:116
  406.2 61.9 %all-to-all-start.3 = ((bf16[4,64,32,224]{3,1,0,2:T(8,128)(2,1)}), bf16[4,64,32,224]{3,1,0,2:T(8,128)(2,1)}, u32[]{:S(2)}, u32[]{:S(2)}) async-start(bf16[4,64,32,224]{3,1,0,2:T(8,128)(2,1)} %copy.95), calls=%async_computation.4 | async-start | bytes 8388608 | tf_op jit(solution)/shard_map/all_to_all | solution.py:109
  487.4 9.0 %copy-start.1 = (bf16[64,64,224]{2,1,0:T(8,128)(2,1)S(1)}, bf16[64,64,224]{2,1,0:T(8,128)(2,1)}, u32[]{:S(2)}) copy-start(bf16[64,64,224]{2,1,0:T(8,128)(2,1)} %param.10) | copy-start | bytes 5505028
Sparse Core Ops, SparseCore 0:
  10.3 126.8 all-gather.1
  293.6 74.1 reduce-scatter.1
where the time goes:
time: 512 us; the launch traced here: 504 us
  waiting for transfers between devices  289 us (56%)
  local copies, waits for them, and re-layouts  112 us (22%)
  matrix products  43.4 us (8%)
  starting transfers between devices  37.2 us (7%)
  between operations  14.5 us (3%)
  other arithmetic  7.9 us (2%)
    all_gather x1, waiting for transfers between devices, shards(): lax.all_gather(grad_output, 'seq', axis=0, tiled=True)  83.7 us
    all_to_all x1, waiting for transfers between devices, shards(): lax.all_to_all(partial_value.astype(jnp.bfloat16), 'seq', split_axis=0, c...  82.1 us
    reduce_scatter x1, waiting for transfers between devices, shards(): lax.psum_scatter(lax.optimization_barrier(packed).astype(jnp.float32).ast...  73.3 us
    all_to_all x1, waiting for transfers between devices, shards(): lax.all_to_all(down_rows.reshape(job_slots, ranks, shard_count, down_slab...  37.3 us
    dot_general x1, matrix products, shards(): lax.dot_general(lax.all_gather(grad_output, 'seq', axis=0, tiled=True), d...  23.3 us
    unnamed x22, local copies, waits for them, and re-layouts  22.9 us
    reshape x2, local copies, waits for them, and re-layouts, shards(): down_rows.reshape(job_slots, ranks, shard_count, down_slab)  15.4 us
    all_to_all x1, waiting for transfers between devices, shards(): lax.all_to_all(adapter_up[chosen], 'seq', split_axis=1, concat_axis=3, ti...  11.5 us
  transfers between devices with their start and end apart: 7, of which 5 were waited for; matrix products, arithmetic and copies ran while one was open for 23% of the time, Pallas kernels for 0%

commit v1 on v0

--- a/solution.py
+++ b/solution.py
@@ -7,8 +7,8 @@
 
 
 def shards(grad_output, hidden, down_weight, adapter_down, adapter_up, job_tenant, job_count):
-    shard_index = lax.axis_index("seq")
-    shard_count = lax.axis_size("seq")
+    shard_index = lax.axis_index(SEQ)
+    shard_count = lax.axis_size(SEQ)
     group_count = lax.axis_size("grp")
     tok_rows = grad_output.shape[0]
     job_slots = job_tenant.shape[1]
@@ -34,8 +34,8 @@
     )
     chosen = job_tenant.T
     fetched_down, fetched_up = (
-        lax.all_to_all(adapter_down[chosen], "seq", split_axis=1, concat_axis=3, tiled=True),
-        lax.all_to_all(adapter_up[chosen], "seq", split_axis=1, concat_axis=3, tiled=True),
+        lax.all_to_all(adapter_down[chosen], SEQ, split_axis=1, concat_axis=3, tiled=True),
+        lax.all_to_all(adapter_up[chosen], SEQ, split_axis=1, concat_axis=3, tiled=True),
     )
     down_stack = fetched_down.reshape(job_slots * ranks, shard_count * down_slab)
     up_stack = fetched_up.reshape(job_slots * ranks, shard_count * up_slab)
@@ -52,31 +52,19 @@
     rank_part = jnp.concatenate([select_jobs(grad_proj), select_jobs(act_proj)], axis=1).astype(
         jnp.bfloat16
     )
+    weight_pair = lax.all_gather(down_weight, "core", axis=0, tiled=True)
+    tokens_same_core = lax.all_gather(grad_output, "chip", axis=0, tiled=True)
     partial_value = lax.dot_general(
-        lax.all_gather(grad_output, "seq", axis=0, tiled=True),
-        down_weight,
-        contract_last,
-        preferred_element_type=jnp.float32,
+        tokens_same_core, weight_pair, contract_last, preferred_element_type=jnp.float32
     )
     routed = lax.all_to_all(
-        partial_value.astype(jnp.bfloat16), "seq", split_axis=0, concat_axis=1, tiled=True
+        partial_value.astype(jnp.bfloat16), "chip", split_axis=0, concat_axis=1, tiled=True
     )
     width_here = routed.shape[1] // group_count
-    packed = jnp.concatenate(
-        [
-            routed.reshape(tok_rows, group_count, width_here),
-            jnp.broadcast_to(rank_part[:, None, :], (tok_rows, group_count, 2 * ranks)),
-        ],
-        axis=2,
-    )
-    summed = lax.psum_scatter(
-        lax.optimization_barrier(packed).astype(jnp.float32).astype(jnp.bfloat16),
-        "grp",
-        scatter_dimension=1,
-        tiled=True,
-    ).astype(jnp.float32)
-    base_grad = summed[:, 0, :width_here].astype(jnp.bfloat16)
-    rank_sum = summed[:, 0, width_here:]
+    base_grad = lax.psum_scatter(
+        routed.reshape(tok_rows, group_count, width_here), "grp", scatter_dimension=1, tiled=True
+    ).reshape(tok_rows, width_here)
+    rank_sum = lax.psum(rank_part.astype(jnp.float32), "grp")
     grad_rank = rank_sum[:, :ranks].astype(jnp.bfloat16)
     act_rank = rank_sum[:, ranks:].astype(jnp.bfloat16)
     grad_spread = (
@@ -108,14 +96,14 @@
     returned_down, returned_up = (
         lax.all_to_all(
             down_rows.reshape(job_slots, ranks, shard_count, down_slab),
-            "seq",
+            SEQ,
             split_axis=2,
             concat_axis=1,
             tiled=True,
         ),
         lax.all_to_all(
             up_rows.reshape(job_slots, ranks, shard_count, up_slab),
-            "seq",
+            SEQ,
             split_axis=2,
             concat_axis=1,
             tiled=True,
@@ -141,13 +129,18 @@
     return (grad_hidden, grad_adapter_down, grad_adapter_up)
 
 
+SEQ = ("chip", "core")
+
+
 def solution(mesh):
+    chips = mesh.devices.reshape(mesh.shape["grp"], mesh.shape["seq"] // 2, 2)
+    mesh = jax.sharding.Mesh(chips, ("grp", "chip", "core"))
     placed = (
-        P("seq", "grp"),
-        P("seq", "grp"),
-        P("seq", "grp"),
-        P(None, None, ("grp", "seq")),
-        P(None, None, ("grp", "seq")),
+        P(SEQ, "grp"),
+        P(SEQ, "grp"),
+        P(SEQ, "grp"),
+        P(None, None, ("grp", "chip", "core")),
+        P(None, None, ("grp", "chip", "core")),
         P(),
         P(),
     )
@@ -155,6 +148,6 @@
         shards,
         mesh=mesh,
         in_specs=placed,
-        out_specs=(P("seq", "grp"), P(None, None, ("grp", "seq")), P(None, None, ("grp", "seq"))),
+        out_specs=(P(SEQ, "grp"), P(None, None, ("grp", "chip", "core")), P(None, None, ("grp", "chip", "core"))),
         check_vma=False,
     )

time: 512 us -> 513 us (level)
  blocking collectives: 0 us -> 107 us
  waiting for transfers between devices: 289 us -> 198 us
  starting transfers between devices: 37.2 us -> 25.6 us
  other arithmetic: 7.9 us -> 0.66 us
    all_to_all x0 -> x1, blocking collectives: none -> 89.2 us  [shards(): lax.all_to_all(partial_value.astype(jnp.bfloat16), 'chip', split_axis=0,...]
    reduce_scatter x1, waiting for transfers between devices: 73.3 us -> 0.01 us  [shards(): lax.psum_scatter(routed.reshape(tok_rows, group_count, width_here), 'grp'...]
    all_to_all x4 -> x3, waiting for transfers between devices: 93.6 us -> 54.1 us  [the longest x1 46.2 us: shards(): lax.all_to_all(adapter_down[chosen], SEQ, split_axis=1, concat_axis=3, ti...]
    psum x0 -> x1, blocking collectives: none -> 17.6 us  [shards(): rank_sum = lax.psum(rank_part.astype(jnp.float32), 'grp')]
    all_gather x1 -> x2, waiting for transfers between devices: 83.7 us -> 98.2 us  [the longest x1 74.1 us: shards(): tokens_same_core = lax.all_gather(grad_output, 'chip', axis=0, tiled=True)]
    all_to_all x4 -> x3, starting transfers between devices: 28.8 us -> 17.7 us  [the longest x1 6.59 us: shards(): lax.all_to_all(adapter_down[chosen], SEQ, split_axis=1, concat_axis=3, ti...]
    reshape x0 -> x1, local copies, waits for them, and re-layouts: none -> 9.97 us  [shards(): routed.reshape(tok_rows, group_count, width_here)]
    all_to_all x1, waiting for transfers between devices: 37.3 us -> 44.4 us  [shards(): lax.all_to_all(down_rows.reshape(job_slots, ranks, shard_count, down_slab...]
  transfers between devices with their start and end apart: 7 -> 7, of which waited for: 5 -> 5; matrix products, arithmetic and copies ran while one was open for 23% -> 22% of each run, Pallas kernels for 0% -> 0%
where the time goes in v1:
time: 513 us; the launch traced here: 504 us
  waiting for transfers between devices  198 us (39%)
  local copies, waits for them, and re-layouts  117 us (23%)
  blocking collectives  107 us (21%)
  matrix products  42.2 us (8%)
  starting transfers between devices  25.6 us (5%)
  between operations  14.2 us (3%)
    all_to_all x1, blocking collectives, shards(): lax.all_to_all(partial_value.astype(jnp.bfloat16), 'chip', split_axis=0,...  89.2 us
    all_gather x1, waiting for transfers between devices, shards(): tokens_same_core = lax.all_gather(grad_output, 'chip', axis=0, tiled=True)  74.1 us
    all_to_all x1, waiting for transfers between devices, shards(): lax.all_to_all(adapter_down[chosen], SEQ, split_axis=1, concat_axis=3, ti...  46.2 us
    all_to_all x1, waiting for transfers between devices, shards(): lax.all_to_all(down_rows.reshape(job_slots, ranks, shard_count, down_slab...  44.4 us
    all_gather x1, waiting for transfers between devices, shards(): weight_pair = lax.all_gather(down_weight, 'core', axis=0, tiled=True)  24.1 us
    dot_general x1, matrix products, shards(): lax.dot_general(tokens_same_core, weight_pair, contract_last, preferred_e...  21.3 us
    unnamed x23, local copies, waits for them, and re-layouts  20.5 us
    psum x1, blocking collectives, shards(): rank_sum = lax.psum(rank_part.astype(jnp.float32), 'grp')  17.6 us
  transfers between devices with their start and end apart: 7, of which 5 were waited for; matrix products, arithmetic and copies ran while one was open for 22% of the time, Pallas kernels for 0%

profile of v1, /device:TPU:32, one launch (start us, length us, event | category | flops | bytes accessed | tf_op | source)
XLA Modules:
  0.0 504.4 jit_solution(12234305566538353482)
XLA Ops:
  8.7 24.1 %all-gather.5.cloned.1.call-done = bf16[1792,2048]{1,0:T(8,128)(2,1)} async-done(((bf16[896,2048]{1,0:T(8,128)(2,1)}), bf16[1792,2048]{1,0:T(8,128)(2,1)}) %all-gather.5.cloned.1.call-update) | async-done | bytes 7340048 | tf_op jit(solution)/shard_map/all_gather | solution.py:55
  32.8 74.1 %all-gather.3.cloned.1.call-done = bf16[2048,2048]{1,0:T(8,128)(2,1)} async-done(((bf16[128,2048]{1,0:T(8,128)(2,1)}), bf16[2048,2048]{1,0:T(8,128)(2,1)}) %all-gather.3.cloned.1.call-update) | async-done | bytes 8388624 | tf_op jit(solution)/shard_map/all_gather | solution.py:56
  106.9 21.3 %convolution_convert_fusion = bf16[2048,1792]{1,0:T(8,128)(2,1)} fusion(bf16[2048,2048]{1,0:T(8,128)(2,1)} %all-gather.3.cloned.1.call-done, bf16[1792,2048]{1,0:T(8,128)(2,1)} %all-gather.5.cloned.1.call-done), kind=kOutput, calls=%fused_computation.7 | convolution fusion | flops 15036055552 | bytes 23068672 | tf_op jit(solution)/shard_map/dot_general | solution.py:57
  128.2 10.0 %copy.60 = bf16[16,128,1792]{1,2,0:T(8,128)(2,1)} copy(bf16[16,128,1792]{2,1,0:T(8,128)(2,1)} %bitcast.111) | data formatting | bytes 14680064 | tf_op jit(solution)/shard_map/all_to_all | solution.py:60
  138.1 89.2 %all_to_all.76 = bf16[16,128,1792]{1,2,0:T(8,128)(2,1)} all-to-all(bf16[16,128,1792]{1,2,0:T(8,128)(2,1)} %copy.60), channel_id=1, replica_groups=mesh['grp'=4,'chip'=16,'core'=2] {'chip'}, dimensions={0} | all-to-all | bytes 14680064 | tf_op jit(solution)/shard_map/all_to_all | solution.py:60
  227.4 10.0 %copy.61 = bf16[128,4,7168]{2,0,1:T(8,128)(2,1)} copy(bf16[128,4,7168]{0,2,1:T(8,128)(2,1)} %bitcast.104) | data formatting | bytes 14680064 | tf_op jit(solution)/shard_map/reshape | solution.py:65
  243.9 4.8 reshape.160
  248.7 5.9 %all-to-all-start.1 = ((bf16[32,2,8192]{2,1,0:T(2,128)(2,1)}), bf16[32,2,8192]{2,1,0:T(2,128)(2,1)S(1)}, u32[]{:S(2)}, u32[]{:S(2)}) async-start(bf16[32,2,8192]{2,1,0:T(2,128)(2,1)} %reshape.160), calls=%async_computation.2 | async-start | bytes 2097152 | tf_op jit(solution)/shard_map/all_to_all | solution.py:38
  257.4 4.8 copy.65
  262.2 7.9 %all-to-all-done.1 = bf16[32,2,8192]{2,1,0:T(2,128)(2,1)S(1)} async-done(((bf16[32,2,8192]{2,1,0:T(2,128)(2,1)}), bf16[32,2,8192]{2,1,0:T(2,128)(2,1)S(1)}, u32[]{:S(2)}, u32[]{:S(2)}) %all-to-all-start.1) | async-done | bytes 1048608 | tf_op jit(solution)/shard_map/all_to_all | solution.py:38
  270.1 6.6 %all-to-all-start.2 = ((bf16[4,32,64,224]{3,2,0,1:T(8,128)(2,1)}), bf16[4,32,64,224]{3,2,0,1:T(8,128)(2,1)}, u32[]{:S(2)}, u32[]{:S(2)}) async-start(bf16[4,32,64,224]{3,2,0,1:T(8,128)(2,1)} %copy.65), calls=%async_computation.3 | async-start | bytes 8388608 | tf_op jit(solution)/shard_map/all_to_all | solution.py:37
  284.5 46.2 %all-to-all-done.2 = bf16[4,32,64,224]{3,2,0,1:T(8,128)(2,1)} async-done(((bf16[4,32,64,224]{3,2,0,1:T(8,128)(2,1)}), bf16[4,32,64,224]{3,2,0,1:T(8,128)(2,1)}, u32[]{:S(2)}, u32[]{:S(2)}) %all-to-all-start.2) | async-done | bytes 3670048 | tf_op jit(solution)/shard_map/all_to_all | solution.py:37
  330.8 6.6 %copy.66 = bf16[4,1,64,32,224]{4,3,2,0,1:T(8,128)(2,1)} copy(bf16[4,1,64,32,224]{4,2,0,3,1:T(8,128)(2,1)} %bitcast.16) | data formatting | bytes 7340032 | tf_op jit(solution)/shard_map/all_to_all | solution.py:37
  337.4 9.0 %reshape.130 = bf16[256,7168]{1,0:T(8,128)(2,1)} reshape(bf16[4,1,64,32,224]{4,3,2,0,1:T(8,128)(2,1)} %copy.66) | data formatting | bytes 7340032 | tf_op jit(solution)/shard_map/reshape | solution.py:40
  349.5 17.6 %psum.7 = bf16[128,128]{0,1:T(8,128)(2,1)S(1)} all-reduce(f32[128,128]{0,1:T(8,128)S(1)} %maximum_convert_fusion), channel_id=1, replica_groups=mesh['grp'=4,'chip'=16,'core'=2] {'grp'}, use_global_device_ids=true, to_apply=%region_4.5 | all-reduce | flops 16384 | bytes 98304 | tf_op jit(solution)/shard_map/psum | solution.py:67
  378.9 5.2 %all-to-all-start.4 = ((bf16[32,2,8192]{2,1,0:T(2,128)(2,1)}), bf16[32,2,8192]{2,1,0:T(2,128)(2,1)S(1)}, u32[]{:S(2)}, u32[]{:S(2)}) async-start(bf16[32,2,8192]{2,1,0:T(2,128)(2,1)} %reshape.162), calls=%async_computation.5 | async-start | bytes 2097152 | tf_op jit(solution)/shard_map/all_to_all | solution.py:104
  387.1 8.8 %reshape.132 = bf16[4,64,32,224]{3,2,1,0:T(8,128)(2,1)} reshape(bf16[4,64,7168]{2,1,0:T(8,128)(2,1)} %fusion) | data formatting | bytes 7340032 | tf_op jit(solution)/shard_map/reshape | solution.py:98
  395.9 6.6 %copy.67 = bf16[4,64,32,224]{3,1,0,2:T(8,128)(2,1)} copy(bf16[4,64,32,224]{3,2,1,0:T(8,128)(2,1)} %reshape.132) | data formatting | bytes 7340032 | tf_op jit(solution)/shard_map/reshape | solution.py:98
  402.5 7.8 %all-to-all-start.3 = ((bf16[4,64,32,224]{3,1,0,2:T(8,128)(2,1)}), bf16[4,64,32,224]{3,1,0,2:T(8,128)(2,1)}, u32[]{:S(2)}, u32[]{:S(2)}) async-start(bf16[4,64,32,224]{3,1,0,2:T(8,128)(2,1)} %copy.67), calls=%async_computation.4 | async-start | bytes 8388608 | tf_op jit(solution)/shard_map/all_to_all | solution.py:97
  420.1 44.4 %all-to-all-done.3 = bf16[4,64,32,224]{3,1,0,2:T(8,128)(2,1)} async-done(((bf16[4,64,32,224]{3,1,0,2:T(8,128)(2,1)}), bf16[4,64,32,224]{3,1,0,2:T(8,128)(2,1)}, u32[]{:S(2)}, u32[]{:S(2)}) %all-to-all-start.3) | async-done | bytes 3670048 | tf_op jit(solution)/shard_map/all_to_all | solution.py:97
  464.4 4.8 copy.68
  469.2 8.5 %reshape.133 = bf16[128,14336]{1,0:T(8,128)(2,1)} reshape(bf16[4,32,64,1,224]{4,2,1,0,3:T(8,128)(2,1)} %copy.68) | data formatting | bytes 7340032 | tf_op jit(solution)/shard_map/reshape | solution.py:119
  477.8 6.0 %copy.69 = bf16[14336,128]{1,0:T(8,128)(2,1)} copy(bf16[14336,128]{0,1:T(8,128)(2,1)} %bitcast.107) | data formatting | bytes 7340032 | tf_op jit(solution)/shard_map/dot_general | solution.py:117
  492.7 5.0 fusion.2
  (68 shorter events, 54.9 us)
Async XLA Ops:
  7.2 247.4 %copy-start = (bf16[64,64,224]{2,1,0:T(8,128)(2,1)S(1)}, bf16[64,64,224]{2,1,0:T(8,128)(2,1)}, u32[]{:S(2)}) copy-start(bf16[64,64,224]{2,1,0:T(8,128)(2,1)} %param.10) | copy-start | bytes 5505028
  7.2 25.6 %all-gather.5.cloned.1.call-start = ((), (), s32[]{:S(2)}) async-start(), calls=%async_computation.7 | async-start | bytes 11010048 | tf_op jit(solution)/shard_map/all_gather | solution.py:55
  7.9 99.0 %all-gather.3.cloned.1.call-start = ((), (), s32[]{:S(2)}) async-start(), calls=%async_computation.6 | async-start | bytes 8912896 | tf_op jit(solution)/shard_map/all_gather | solution.py:56
  8.7 484.0 %reduce-scatter.2.cloned.1.call-start = ((), (), s32[]{:S(2)}) async-start(), calls=%async_computation.8 | async-start | bytes 9175040 | tf_op jit(solution)/shard_map/reduce_scatter | solution.py:64
  237.3 0.7 copy-start.6
  237.3 1.2 copy-start.5
  248.7 21.5 %all-to-all-start.1 = ((bf16[32,2,8192]{2,1,0:T(2,128)(2,1)}), bf16[32,2,8192]{2,1,0:T(2,128)(2,1)S(1)}, u32[]{:S(2)}, u32[]{:S(2)}) async-start(bf16[32,2,8192]{2,1,0:T(2,128)(2,1)} %reshape.160), calls=%async_computation.2 | async-start | bytes 2097152 | tf_op jit(solution)/shard_map/all_to_all | solution.py:38
  262.2 14.5 %copy-start.7 = (s32[32,4]{0,1:T(4,128)S(1)}, s32[32,4]{0,1:T(4,128)}, u32[]{:S(2)}) copy-start(s32[32,4]{0,1:T(4,128)} %param.13) | copy-start | bytes 1540
  270.1 60.6 %all-to-all-start.2 = ((bf16[4,32,64,224]{3,2,0,1:T(8,128)(2,1)}), bf16[4,32,64,224]{3,2,0,1:T(8,128)(2,1)}, u32[]{:S(2)}, u32[]{:S(2)}) async-start(bf16[4,32,64,224]{3,2,0,1:T(8,128)(2,1)} %copy.65), calls=%async_computation.3 | async-start | bytes 8388608 | tf_op jit(solution)/shard_map/all_to_all | solution.py:37
  279.1 3.8 copy-start.4
  337.4 9.0 %copy-start.2 = (bf16[128,7168]{1,0:T(8,128)(2,1)S(1)}, bf16[128,7168]{1,0:T(8,128)(2,1)}, u32[]{:S(2)}) copy-start(bf16[128,7168]{1,0:T(8,128)(2,1)} %param.8) | copy-start | bytes 5505028
  374.1 10.0 %copy-start.3 = (bf16[128,7168]{1,0:T(8,128)(2,1)S(1)}, bf16[128,7168]{1,0:T(8,128)(2,1)}, u32[]{:S(2)}) copy-start(bf16[128,7168]{1,0:T(8,128)(2,1)} %param.8) | copy-start | bytes 5505028
  378.9 23.7 %all-to-all-start.4 = ((bf16[32,2,8192]{2,1,0:T(2,128)(2,1)}), bf16[32,2,8192]{2,1,0:T(2,128)(2,1)S(1)}, u32[]{:S(2)}, u32[]{:S(2)}) async-start(bf16[32,2,8192]{2,1,0:T(2,128)(2,1)} %reshape.162), calls=%async_computation.5 | async-start | bytes 2097152 | tf_op jit(solution)/shard_map/all_to_all | solution.py:104
  402.5 61.9 %all-to-all-start.3 = ((bf16[4,64,32,224]{3,1,0,2:T(8,128)(2,1)}), bf16[4,64,32,224]{3,1,0,2:T(8,128)(2,1)}, u32[]{:S(2)}, u32[]{:S(2)}) async-start(bf16[4,64,32,224]{3,1,0,2:T(8,128)(2,1)} %copy.67), calls=%async_computation.4 | async-start | bytes 8388608 | tf_op jit(solution)/shard_map/all_to_all | solution.py:97
  492.7 5.0 copy-start.1
Sparse Core Ops, SparseCore 0:
  9.7 23.0 all-gather.4
  34.9 71.9 all-gather.2
  237.5 72.3 reduce-scatter.1
